TPU v7x, 32 devices: a whole 2x2x4 slice. The times are simulated.
32 devices in a mesh: dp: 8 (over z, y), expert: 4 (over x, core).
Axes of the slice: x: 2, y: 2, z: 4, core: 2. Of those that a mesh axis runs over, the one named last changes fastest.
Arguments:
- residual: bfloat16 [4096, 3072], P(('dp', 'expert')), may hold values from -36 to 36
- context: bfloat16 [4096, 24, 128], P('dp', 'expert'), may hold values from -6 to 6
- master: float32 [24, 128, 3072], P('expert', 'dp'), may hold values from -0.109375 to 0.109375
- grad: float32 [24, 128, 3072], P('expert', 'dp'), may hold values from -6 to 6
- moment: float32 [24, 128, 3072], P('expert', 'dp'), may hold values from -1.8 to 1.8
- second: float32 [24, 128, 3072], P('expert', 'dp'), may hold values from 0.0005 to 0.02
- gain: float32 [3072], replicated, may hold values from 0.5 to 1.5
- token_ids: int32 [4096], P(('dp', 'expert')), may hold values from 0 to 51199
- table_one: int32 [51200], replicated, may hold values from 0 to 7
- table_two: int32 [51200], replicated, may hold values from 0 to 7
- w_in: bfloat16 [8, 1536, 5120], P('dp', None, 'expert'), may hold values from -0.15625 to 0.15625
- w_out: bfloat16 [8, 5120, 1536], P('dp', 'expert'), may hold values from -0.078125 to 0.078125
Outputs:
- mixed: bfloat16 [4096, 3072], P(('dp', 'expert'))
All inputs are finite; a program needn't handle non-finite values.
Results may differ from a plain program's by a relative error of at most 0.009.
Values may be sent and summed in bfloat16 or wider, within the bound.
A program may use at most 64 MiB of HBM per device.

v0:
```python
import jax
import jax.numpy as jnp
from jax import lax
from jax.sharding import PartitionSpec as P

lr_rate = 0.01
beta_one = 0.9
beta_two = 0.999
adam_step = 10.0
eps_adam = 1e-08
eps_norm = 1e-05


def adam_weight(master, grad, moment, second):
    new_moment = beta_one * moment + (1.0 - beta_one) * grad
    new_second = beta_two * second + (1.0 - beta_two) * grad * grad
    corr_one = 1.0 - beta_one**adam_step
    corr_two = 1.0 - beta_two**adam_step
    update = new_moment / corr_one / (jnp.sqrt(new_second / corr_two) + eps_adam)
    return (master - lr_rate * update).astype(jnp.bfloat16)


def slot_tables(routes_of, experts, capacity):
    onehot = (routes_of[..., None] == jnp.arange(experts, dtype=jnp.int32)).astype(jnp.int32)
    before = jnp.cumsum(onehot, axis=-2) - onehot
    slot_rank = jnp.sum(before * onehot, axis=-1)
    match_expert = routes_of[..., None, :] == jnp.arange(experts, dtype=jnp.int32)[:, None]
    match_slot = slot_rank[..., None, :] == jnp.arange(capacity, dtype=jnp.int32)[:, None]
    return (match_expert[..., :, None, :] & match_slot[..., None, :, :]).astype(jnp.bfloat16)


def on_device(
    residual,
    context,
    master,
    grad,
    moment,
    second,
    gain,
    token_ids,
    table_one,
    table_two,
    w_in,
    w_out,
):
    experts = lax.axis_size("dp") * w_in.shape[0]
    tok_count = residual.shape[0]
    model_width = residual.shape[1]
    half_width = model_width // 2
    capacity = max(2, 5 * tok_count // (4 * experts))
    fresh = adam_weight(master, grad, moment, second)
    weight_all = lax.all_gather(fresh, "dp", axis=1, tiled=True)
    weight_rows = weight_all.reshape(-1, model_width)
    ctx_rows = context.reshape(context.shape[0], -1)
    attn = lax.psum_scatter(
        jnp.dot(ctx_rows, weight_rows, preferred_element_type=jnp.float32).astype(jnp.bfloat16),
        "expert",
        scatter_dimension=0,
        tiled=True,
    ).astype(jnp.float32)
    state = residual.astype(jnp.float32) + attn
    scale = lax.rsqrt(jnp.mean(state * state, axis=-1, keepdims=True) + eps_norm)
    normed = (state * scale * gain).astype(jnp.bfloat16)
    halves = normed.reshape(tok_count, 2, half_width)
    routes = jnp.stack([table_one[token_ids], table_two[token_ids]])
    dispatch = slot_tables(routes, experts, capacity)
    outgoing = jnp.einsum(
        "kest,tkd->eksd", dispatch, halves, preferred_element_type=jnp.float32
    ).astype(jnp.bfloat16)
    arrived = lax.all_to_all(outgoing, "dp", split_axis=0, concat_axis=0, tiled=True)
    rows_here = arrived.reshape(-1, half_width)
    inner = jnp.dot(
        lax.all_gather(rows_here, "expert", axis=0, tiled=True),
        w_in[0],
        preferred_element_type=jnp.float32,
    )
    hidden = jax.nn.gelu(inner, approximate=True).astype(jnp.bfloat16)
    partial_rows = jnp.dot(hidden, w_out[0], preferred_element_type=jnp.float32)
    expert_out = lax.psum_scatter(
        partial_rows.astype(jnp.bfloat16), "expert", scatter_dimension=0, tiled=True
    )
    shaped = expert_out.reshape(experts, 2, capacity, half_width)
    returned = lax.all_to_all(shaped, "dp", split_axis=0, concat_axis=0, tiled=True)
    routed = jnp.einsum("kest,eksd->tkd", dispatch, returned, preferred_element_type=jnp.float32)
    routed = routed.reshape(tok_count, model_width)
    return (state + routed).astype(jnp.bfloat16)


def solution(mesh):
    return jax.shard_map(
        on_device,
        mesh=mesh,
        in_specs=(
            P(("dp", "expert"), None),
            P("dp", "expert", None),
            P("expert", "dp", None),
            P("expert", "dp", None),
            P("expert", "dp", None),
            P("expert", "dp", None),
            P(),
            P(("dp", "expert")),
            P(),
            P(),
            P("dp", None, "expert"),
            P("dp", "expert", None),
        ),
        out_specs=P(("dp", "expert"), None),
        check_vma=False,
    )
```

profile of v0, /device:TPU:0, one launch (start us, length us, event | category | flops | bytes accessed | tf_op | source)
XLA Modules:
  0.0 305.8 jit_solution(10959827821337791206)
XLA Ops:
  6.5 0.0 copy-start
  6.5 0.0 all-gather.3.cloned.1.call-start
  6.5 4.0 %fusion.25 = bf16[6,16,3072]{2,1,0:T(8,128)(2,1)} fusion(f32[6,16,3072]{2,1,0:T(8,128)} %param.14, f32[6,16,3072]{2,1,0:T(8,128)} %param.15, f32[6,16,3072]{2,1,0:T(8,128)} %param.17, f32[6,16,3072]{2,1,0:T(8,128)} %param.16), kind=kLoop, calls=%fused_computation.34 | loop fusion | flops 4128768 | bytes 5308416 | tf_op jit(solution)/shard_map/convert_element_type | solution.py:20
  10.6 0.0 all-gather.3.cloned.1.call-update
  10.6 0.0 reduce-scatter.7.cloned.1.call-start
  10.7 82.2 %all-gather.3.cloned.1.call-done = bf16[6,128,3072]{2,1,0:T(8,128)(2,1)} async-done(((bf16[6,16,3072]{2,1,0:T(8,128)(2,1)}), bf16[6,128,3072]{2,1,0:T(8,128)(2,1)}) %all-gather.3.cloned.1.call-update) | async-done | bytes 4718608 | tf_op jit(solution)/shard_map/all_gather | solution.py:52
  92.8 0.0 copy-done
  92.8 6.4 %fusion.8 = bf16[512,3072]{0,1:T(8,128)(2,1)} fusion(bf16[6,128,3072]{2,1,0:T(8,128)(2,1)} %all-gather.3.cloned.1.call-done, bf16[512,6,128]{2,0,1:T(8,128)(2,1)S(1)} %copy-done), kind=kOutput, calls=%fused_computation.13 | convolution fusion | flops 2417491968 | bytes 8650752 | tf_op jit(solution)/shard_map/dot_general | solution.py:56
  99.3 4.6 %copy.33 = bf16[512,3072]{1,0:T(8,128)(2,1)} copy(bf16[512,3072]{0,1:T(8,128)(2,1)} %fusion.8) | data formatting | bytes 6291456
  103.9 0.0 copy-start.6
  103.9 0.0 copy-start.1
  103.9 0.0 copy-start.2
  103.9 0.0 copy-start.3
  103.9 0.0 reduce-scatter.7.cloned.1.call-update
  104.0 0.0 all-gather.5.cloned.1.call-start
  104.0 0.6 copy-done.6
  104.6 0.3 copy-done.1
  104.9 1.1 gather_fusion.1
  106.0 0.0 copy-done.2
  106.0 1.1 gather_fusion
  107.2 0.0 copy-done.3
  107.2 0.4 copy.22
  107.6 0.1 fusion.28
  107.7 0.2 reduce_window_sum.11
  107.9 0.2 select_reduce_fusion
  108.1 0.0 copy-start.4
  108.1 32.2 %reduce-scatter.7.cloned.1.call-done = bf16[128,3072]{1,0:T(8,128)(2,1)} async-done(((bf16[512,3072]{1,0:T(8,128)(2,1)}), bf16[128,3072]{1,0:T(8,128)(2,1)}) %reduce-scatter.7.cloned.1.call-update) | async-done | bytes 786448
  140.3 1.5 copy.34
  141.9 0.4 multiply_reduce_fusion
  142.3 0.0 copy-done.4
  142.3 0.5 multiply_convert_fusion
  142.8 0.5 fusion.14
  143.3 1.0 copy.24
  144.3 29.6 %all_to_all.10 = bf16[8,2,20,1536]{3,1,2,0:T(2,128)(2,1)S(1)} all-to-all(bf16[8,2,20,1536]{3,1,2,0:T(2,128)(2,1)S(1)} %copy.24), channel_id=1, replica_groups=mesh['dp'=8,'expert'=4] {'dp'}, dimensions={0} | all-to-all | bytes 1966080 | tf_op jit(solution)/shard_map/all_to_all | solution.py:70
  173.9 0.1 copy.25
  174.0 1.1 reshape.33
  175.1 0.0 all-gather.5.cloned.1.call-update
  175.2 0.2 reduce-scatter.5.cloned.1.call-start
  175.4 30.9 %all-gather.5.cloned.1.call-done = bf16[1280,1536]{1,0:T(8,128)(2,1)} async-done(((bf16[320,1536]{1,0:T(8,128)(2,1)}), bf16[1280,1536]{1,0:T(8,128)(2,1)}) %all-gather.5.cloned.1.call-update) | async-done | bytes 3932176 | tf_op jit(solution)/shard_map/all_gather | solution.py:73
  206.2 0.0 copy-start.5
  206.2 9.1 %fusion.7 = bf16[1280,1280]{1,0:T(8,128)(2,1)S(1)} fusion(bf16[1280,1536]{1,0:T(8,128)(2,1)} %all-gather.5.cloned.1.call-done, bf16[1,1536,1280]{2,1,0:T(8,128)(2,1)} %param.22), kind=kOutput, calls=%fused_computation.11 | convolution fusion | flops 5047910400 | bytes 11141120 | tf_op jit(solution)/shard_map/dot_general | solution.py:72
  215.3 0.0 copy-done.5
  215.4 6.8 %convolution_convert_fusion = bf16[1280,1536]{1,0:T(8,128)(2,1)} fusion(bf16[1280,1280]{1,0:T(8,128)(2,1)S(1)} %fusion.7, bf16[1,1280,1536]{2,1,0:T(8,128)(2,1)S(1)} %copy-done.5), kind=kOutput, calls=%fused_computation.3 | convolution fusion | flops 5035130880 | bytes 11141120 | tf_op jit(solution)/shard_map/dot_general | solution.py:78
  222.2 0.0 reduce-scatter.5.cloned.1.call-update
  222.2 43.1 %reduce-scatter.5.cloned.1.call-done = bf16[320,1536]{1,0:T(8,128)(2,1)} async-done(((bf16[1280,1536]{1,0:T(8,128)(2,1)}), bf16[320,1536]{1,0:T(8,128)(2,1)}) %reduce-scatter.5.cloned.1.call-update) | async-done | bytes 983056 | tf_op jit(solution)/shard_map/reduce_scatter | solution.py:79
  265.3 1.3 reshape.34
  266.6 0.8 copy.26
  267.3 29.6 %all_to_all.11 = bf16[8,2,20,1536]{3,1,2,0:T(2,128)(2,1)S(1)} all-to-all(bf16[8,2,20,1536]{3,1,2,0:T(2,128)(2,1)S(1)} %copy.26), channel_id=1, replica_groups=mesh['dp'=8,'expert'=4] {'dp'}, dimensions={0} | all-to-all | bytes 1966080 | tf_op jit(solution)/shard_map/all_to_all | solution.py:83
  297.0 0.8 fusion.23
  297.8 0.3 fusion.15
  298.0 1.2 copy.28
  (6 shorter events, 0.0 us)
Async XLA Ops:
  6.5 86.3 %copy-start = (bf16[512,6,128]{2,0,1:T(8,128)(2,1)S(1)}, bf16[512,6,128]{2,0,1:T(8,128)(2,1)}, u32[]{:S(2)}) copy-start(bf16[512,6,128]{2,0,1:T(8,128)(2,1)} %param.13) | copy-start | bytes 2359300
  6.5 86.3 %all-gather.3.cloned.1.call-start = ((), (), s32[]{:S(2)}) async-start(), calls=%async_computation.4 | async-start | bytes 5308416 | tf_op jit(solution)/shard_map/all_gather | solution.py:52
  10.6 129.7 %reduce-scatter.7.cloned.1.call-start = ((), (), s32[]{:S(2)}) async-start(), calls=%async_computation.7 | async-start | bytes 3932160
  103.9 0.7 copy-start.6
  103.9 0.9 copy-start.1
  103.9 2.1 copy-start.2
  103.9 3.3 %copy-start.3 = (bf16[128,3072]{1,0:T(8,128)(2,1)S(1)}, bf16[128,3072]{1,0:T(8,128)(2,1)}, u32[]{:S(2)}) copy-start(bf16[128,3072]{1,0:T(8,128)(2,1)} %param.12) | copy-start | bytes 2359300
  104.0 102.3 %all-gather.5.cloned.1.call-start = ((), (), s32[]{:S(2)}) async-start(), calls=%async_computation.5 | async-start | bytes 4915200 | tf_op jit(solution)/shard_map/all_gather | solution.py:73
  108.1 34.2 %copy-start.4 = (f32[3072]{0:T(1024)S(1)}, f32[3072]{0:T(1024)}, u32[]{:S(2)}) copy-start(f32[3072]{0:T(1024)} %param.18) | copy-start | bytes 36868
  175.2 90.1 %reduce-scatter.5.cloned.1.call-start = ((), (), s32[]{:S(2)}) async-start(), calls=%async_computation.6 | async-start | bytes 4915200 | tf_op jit(solution)/shard_map/reduce_scatter | solution.py:79
  206.2 9.1 %copy-start.5 = (bf16[1,1280,1536]{2,1,0:T(8,128)(2,1)S(1)}, bf16[1,1280,1536]{2,1,0:T(8,128)(2,1)}, u32[]{:S(2)}) copy-start(bf16[1,1280,1536]{2,1,0:T(8,128)(2,1)} %param.23) | copy-start | bytes 11796484
Sparse Core Ops, SparseCore 0:
  10.7 82.0 all-gather.2
  104.1 36.2 reduce-scatter.6
  175.3 30.9 all-gather.4
  222.3 42.8 reduce-scatter.4
where the time goes:
time: 306 us
  waiting for transfers between devices  188 us (61%)
  blocking collectives  59.2 us (19%)
  matrix products  23.6 us (8%)
  local copies, waits for them, and re-layouts  15.1 us (5%)
  between operations  13.3 us (4%)
  other arithmetic  5.76 us (2%)
    all_gather x1, waiting for transfers between devices, on_device(): weight_all = lax.all_gather(fresh, 'dp', axis=1, tiled=True)  82.2 us
    reduce_scatter x1, waiting for transfers between devices, on_device(): lax.psum_scatter(partial_rows.astype(jnp.bfloat16), 'expert', scatter_dim...  43.1 us
    unnamed x5, waiting for transfers between devices  32.3 us
    all_gather x1, waiting for transfers between devices, on_device(): lax.all_gather(rows_here, 'expert', axis=0, tiled=True)  30.9 us
    all_to_all x1, blocking collectives, on_device(): lax.all_to_all(shaped, 'dp', split_axis=0, concat_axis=0, tiled=True)  29.6 us
    all_to_all x1, blocking collectives, on_device(): lax.all_to_all(outgoing, 'dp', split_axis=0, concat_axis=0, tiled=True)  29.6 us
    dot_general x1, matrix products, on_device(): jnp.dot(lax.all_gather(rows_here, 'expert', axis=0, tiled=True), w_in[0],...  9.09 us
    unnamed x17, local copies, waits for them, and re-layouts  7.39 us
  transfers between devices with their start and end apart: 4, of which 4 were waited for; matrix products, arithmetic and copies ran while one was open for 1% of the time, Pallas kernels for 0%

commit v1 on v0

--- a/solution.py
+++ b/solution.py
@@ -1,6 +1,10 @@
+import functools
+
 import jax
 import jax.numpy as jnp
 from jax import lax
+from jax.experimental import pallas as pl
+from jax.experimental.pallas import tpu as pltpu
 from jax.sharding import PartitionSpec as P
 
 lr_rate = 0.01
@@ -9,6 +13,8 @@
 adam_step = 10.0
 eps_adam = 1e-08
 eps_norm = 1e-05
+
+MESH = pl.DeviceIdType.MESH
 
 
 def adam_weight(master, grad, moment, second):
@@ -29,25 +35,334 @@
     return (match_expert[..., :, None, :] & match_slot[..., None, :, :]).astype(jnp.bfloat16)
 
 
-def on_device(
-    residual,
-    context,
-    master,
-    grad,
-    moment,
-    second,
-    gain,
-    token_ids,
-    table_one,
-    table_two,
-    w_in,
-    w_out,
+def remote(src, dst, send_sem, recv_sem, where):
+    return pltpu.make_async_remote_copy(
+        src_ref=src, dst_ref=dst, send_sem=send_sem, recv_sem=recv_sem,
+        device_id=where, device_id_type=MESH,
+    )
+
+
+def greet(partners):
+    barrier = pltpu.get_barrier_semaphore()
+    for where in partners:
+        pl.semaphore_signal(barrier, inc=1, device_id=where, device_id_type=MESH)
+    pl.semaphore_wait(barrier, len(partners))
+
+
+def proj_kernel(
+    n, width, exp_size, chunk,
+    master, grad, moment, second, ctx, resid, gain,
+    state, normed,
+    wbuf, own, snd, prec, xsnd, xrec,
+    sz, rz, sy, ry, sp, rp, sx, rx,
 ):
-    experts = lax.axis_size("dp") * w_in.shape[0]
-    tok_count = residual.shape[0]
+    chunks = width // chunk
+    far, chips = n // 2, exp_size // 2
+    heads, _, rows = wbuf.shape[1:4]
+    tok = resid.shape[0]
+    d, e = lax.axis_index("dp"), lax.axis_index("expert")
+    a, b, x, c = d // 2, d % 2, e // 2, e % 2
+    mate = (d, x * 2 + 1 - c)
+    pair = (a * 2 + 1 - b, e)
+
+    def z_dev(j):
+        return (((a + j) % far) * 2 + b, e)
+
+    def x_dev(j):
+        return (d, ((x + j) % chips) * 2 + c)
+
+    greet([z_dev(j) for j in range(1, far)] + [pair, mate] + [x_dev(j) for j in range(1, chips)])
+
+    def z_copy(t, j, whose):
+        spot = wbuf.at[t, :, whose]
+        return remote(spot, spot, sz.at[t, j - 1], rz.at[t, j - 1], z_dev(j))
+
+    def y_copy(t, j, whose):
+        spot = wbuf.at[t, :, whose]
+        return remote(spot, spot, sy.at[t, j], ry.at[t, j], pair)
+
+    def mate_copy(t, xx):
+        return remote(snd.at[t, xx], prec.at[t, xx], sp.at[t, xx], rp.at[t, xx], mate)
+
+    def x_copy(t, j, there):
+        return remote(xsnd.at[t, (x + j) % chips], xrec.at[t, there], sx.at[t, j - 1], rx.at[t, j - 1], x_dev(j))
+
+    def cols(t):
+        return pl.ds(pl.multiple_of(t * chunk, chunk), chunk)
+
+    def stage_send(t):
+        k = cols(t)
+        wbuf[t, :, d] = adam_weight(master[:, :, k], grad[:, :, k], moment[:, :, k], second[:, :, k])
+        for j in range(far - 1, 0, -1):
+            z_copy(t, j, d).start()
+        y_copy(t, 0, d).start()
+
+    def stage_forward(t):
+        for j in range(1, far):
+            whose = ((a - j + far) % far) * 2 + b
+            z_copy(t, j, whose).wait_recv()
+            y_copy(t, j, whose).start()
+
+    def stage_dot(t):
+        for j in range(far):
+            y_copy(t, j, ((a - j + far) % far) * 2 + 1 - b).wait_recv()
+        for side in (1, 0):
+            for j in range(chips):
+                xx = (x + j) % chips
+                block = xx * 2 + (1 - c if side else c)
+                lhs = ctx[pl.ds(pl.multiple_of(block * tok, tok), tok), :]
+                w = wbuf[t].reshape(heads * n * rows, chunk)
+                term = jnp.dot(lhs, w, preferred_element_type=jnp.float32).astype(jnp.bfloat16)
+                if side:
+                    snd[t, xx] = term
+                    mate_copy(t, xx).start()
+                else:
+                    own[t, xx] = term
+
+    def stage_pair(t):
+        for j in range(chips):
+            mate_copy(t, (x + j) % chips).wait_recv()
+        for j in range(1, chips):
+            xx = (x + j) % chips
+            both = own[t, xx].astype(jnp.float32) + prec[t, xx].astype(jnp.float32)
+            xsnd[t, xx] = both.astype(jnp.bfloat16)
+            x_copy(t, j, x).start()
+
+    def stage_state(t):
+        total = own[t, x].astype(jnp.float32) + prec[t, x].astype(jnp.float32)
+        for j in range(1, chips):
+            there = (x - j + chips) % chips
+            x_copy(t, j, there).wait_recv()
+            total = total + xrec[t, there].astype(jnp.float32)
+        state[:, cols(t)] = resid[:, cols(t)].astype(jnp.float32) + total
+
+    def step(t, carry):
+        for lag, stage in ((0, stage_send), (2, stage_forward), (3, stage_dot), (4, stage_pair), (5, stage_state)):
+            @pl.when((t >= lag) & (t < lag + chunks))
+            def _():
+                stage(t - lag)
+        return carry
+
+    lax.fori_loop(0, chunks + 5, step, 0)
+    whole = state[...]
+    scale = lax.rsqrt(jnp.mean(whole * whole, axis=-1, keepdims=True) + eps_norm)
+    normed[...] = (whole * scale * gain[...]).astype(jnp.bfloat16)
+
+    def drain(t, carry):
+        for j in range(1, far):
+            z_copy(t, j, d).wait_send()
+        for j in range(far):
+            y_copy(t, j, ((a - j + far) % far) * 2 + b).wait_send()
+        for j in range(chips):
+            mate_copy(t, (x + j) % chips).wait_send()
+        for j in range(1, chips):
+            x_copy(t, j, x).wait_send()
+        return carry
+
+    lax.fori_loop(0, chunks, drain, 0)
+
+
+def project(n, exp_size, context, residual, master, grad, moment, second, gain):
+    tok, width = residual.shape
+    chunk = min(512, width)
+    chunks = width // chunk
+    heads, rows = master.shape[:2]
+    far, chips = n // 2, exp_size // 2
+    dma = pltpu.SemaphoreType.DMA
+    vmem = pl.BlockSpec(memory_space=pltpu.VMEM)
+    term = pltpu.VMEM((chunks, chips, tok, chunk), jnp.bfloat16)
+    return pl.pallas_call(
+        functools.partial(proj_kernel, n, width, exp_size, chunk),
+        out_shape=(
+            jax.ShapeDtypeStruct((tok, width), jnp.float32),
+            jax.ShapeDtypeStruct((tok, width), jnp.bfloat16),
+        ),
+        in_specs=[vmem] * 7,
+        out_specs=(vmem, vmem),
+        scratch_shapes=[
+            pltpu.VMEM((chunks, heads, n, rows, chunk), jnp.bfloat16),
+            term, term, term, term, term,
+            dma((chunks, far - 1)), dma((chunks, far - 1)),
+            dma((chunks, far)), dma((chunks, far)),
+            dma((chunks, chips)), dma((chunks, chips)),
+            dma((chunks, chips - 1)), dma((chunks, chips - 1)),
+        ],
+        compiler_params=pltpu.CompilerParams(collective_id=0, has_side_effects=True),
+        name="project",
+    )(master, grad, moment, second, context.reshape(context.shape[0], -1), residual, gain.reshape(1, -1))
+
+
+def moe_kernel(
+    n, exp_size,
+    normed, state, pick, place, w_in, w_out,
+    mixed,
+    outg, rows, part, prec, xsnd, xrec, acc, fin, ret,
+    s1, r1, sm, rm, sx, rx, sp, rp, sy, ry, sb, rb,
+):
+    chips = exp_size // 2
+    slots, half = outg.shape[1:]
+    tok = normed.shape[0]
+    d, e = lax.axis_index("dp"), lax.axis_index("expert")
+    x, c = e // 2, e % 2
+    mate = (d, x * 2 + 1 - c)
+
+    def x_dev(j):
+        return (d, ((x + j) % chips) * 2 + c)
+
+    greet([((d + k) % n, e) for k in range(1, n)] + [mate] + [x_dev(j) for j in range(1, chips)])
+
+    def out_copy(k, whose):
+        return remote(outg.at[(d + k) % n], rows.at[whose, e], s1.at[k], r1.at[k], ((d + k) % n, e))
+
+    def wide_copy(k, j, col):
+        s = (d - k + n) % n
+        return remote(rows.at[s, e], rows.at[s, col], sx.at[k, j - 1], rx.at[k, j - 1], x_dev(j))
+
+    def mate_copy(k, j, core):
+        spot = rows.at[(d - k + n) % n, ((x - j + chips) % chips) * 2 + core]
+        return remote(spot, spot, sm.at[k, j], rm.at[k, j], mate)
+
+    def part_copy(k, j):
+        s, xx = (d - k + n) % n, (x + j) % chips
+        return remote(part.at[s, xx * 2 + 1 - c], prec.at[s, xx], sp.at[k, j], rp.at[k, j], mate)
+
+    def sum_copy(k, j, there):
+        s = (d - k + n) % n
+        return remote(xsnd.at[s, (x + j) % chips], xrec.at[s, there], sy.at[k, j - 1], ry.at[k, j - 1], x_dev(j))
+
+    def back_copy(k, whose):
+        s = (d - k + n) % n
+        return remote(fin.at[s], ret.at[whose], sb.at[k], rb.at[k], (s, e))
+
+    picked = jnp.dot(pick[:, :tok], normed[:, :half], preferred_element_type=jnp.float32)
+    picked = picked + jnp.dot(pick[:, tok:], normed[:, half:], preferred_element_type=jnp.float32)
+    outg[...] = picked.reshape(n, slots, half).astype(jnp.bfloat16)
+    for k in range(1, n):
+        out_copy(k, d).start()
+    rows[d, e] = outg[d]
+
+    def stage_forward(k):
+        @pl.when(k > 0)
+        def _():
+            out_copy(k, (d - k + n) % n).wait_recv()
+        for j in range(1, chips):
+            wide_copy(k, j, e).start()
+        mate_copy(k, 0, c).start()
+
+    def stage_mate(k):
+        for j in range(1, chips):
+            wide_copy(k, j, ((x - j + chips) % chips) * 2 + c).wait_recv()
+            mate_copy(k, j, c).start()
+
+    def stage_dot(k):
+        s = (d - k + n) % n
+        for j in range(chips):
+            mate_copy(k, j, 1 - c).wait_recv()
+        block = rows[s].astype(jnp.float32).reshape(exp_size * slots, half).astype(jnp.bfloat16)
+        inner = jnp.dot(block, w_in[...], preferred_element_type=jnp.float32)
+        hidden = jax.nn.gelu(inner, approximate=True).astype(jnp.bfloat16)
+        piece = jnp.dot(hidden, w_out[...], preferred_element_type=jnp.float32)
+        part[s] = piece.reshape(exp_size, slots, half).astype(jnp.bfloat16)
+        for j in range(chips):
+            part_copy(k, j).start()
+
+    def stage_pair(k):
+        s = (d - k + n) % n
+        for j in range(chips):
+            part_copy(k, j).wait_recv()
+        for j in range(chips):
+            xx = (x + j) % chips
+            both = part[s, xx * 2 + c].astype(jnp.float32) + prec[s, xx].astype(jnp.float32)
+            if j:
+                xsnd[s, xx] = both.astype(jnp.bfloat16)
+                sum_copy(k, j, x).start()
+            else:
+                acc[s] = both
+
+    def stage_back(k):
+        s = (d - k + n) % n
+        total = acc[s]
+        for j in range(1, chips):
+            there = (x - j + chips) % chips
+            sum_copy(k, j, there).wait_recv()
+            total = total + xrec[s, there].astype(jnp.float32)
+
+        @pl.when(k > 0)
+        def _():
+            fin[s] = total.astype(jnp.bfloat16)
+            back_copy(k, d).start()
+
+        @pl.when(k == 0)
+        def _():
+            ret[d] = total.astype(jnp.bfloat16)
+
+    def step(t, carry):
+        for lag, stage in ((0, stage_forward), (1, stage_mate), (2, stage_dot), (3, stage_pair), (4, stage_back)):
+            @pl.when((t >= lag) & (t < lag + n))
+            def _():
+                stage(t - lag)
+        return carry
+
+    lax.fori_loop(0, n + 4, step, 0)
+    for k in range(1, n):
+        back_copy(k, (d + k) % n).wait_recv()
+    back = ret[...].astype(jnp.float32).reshape(n * slots, half).astype(jnp.bfloat16)
+    for k in range(2):
+        routed = jnp.dot(place[pl.ds(k * tok, tok), :], back, preferred_element_type=jnp.float32)
+        mixed[:, pl.ds(k * half, half)] = (state[:, pl.ds(k * half, half)] + routed).astype(jnp.bfloat16)
+
+    def drain(k, carry):
+        @pl.when(k > 0)
+        def _():
+            out_copy(k, d).wait_send()
+            back_copy(k, d).wait_send()
+        for j in range(chips):
+            mate_copy(k, j, c).wait_send()
+            part_copy(k, j).wait_send()
+        for j in range(1, chips):
+            wide_copy(k, j, e).wait_send()
+            sum_copy(k, j, x).wait_send()
+        return carry
+
+    lax.fori_loop(0, n, drain, 0)
+
+
+def mix_experts(n, exp_size, capacity, state, normed, routes, w_in, w_out):
+    tok, width = state.shape
+    half, slots, chips = width // 2, 2 * capacity, exp_size // 2
+    dispatch = slot_tables(routes, n, capacity)
+    blank = jnp.zeros_like(dispatch[0])
+    pick = jnp.stack(
+        [jnp.concatenate([dispatch[0], blank], -1), jnp.concatenate([blank, dispatch[1]], -1)], axis=1
+    ).reshape(n * slots, 2 * tok)
+    dma = pltpu.SemaphoreType.DMA
+    vmem = pl.BlockSpec(memory_space=pltpu.VMEM)
+    bf = jnp.bfloat16
+    pairs = pltpu.VMEM((n, chips, slots, half), bf)
+    full = pltpu.VMEM((n, exp_size, slots, half), bf)
+    one = pltpu.VMEM((n, slots, half), bf)
+    return pl.pallas_call(
+        functools.partial(moe_kernel, n, exp_size),
+        out_shape=jax.ShapeDtypeStruct((tok, width), bf),
+        in_specs=[vmem] * 6,
+        out_specs=vmem,
+        scratch_shapes=[
+            one, full, full, pairs, pairs, pairs,
+            pltpu.VMEM((n, slots, half), jnp.float32), one, one,
+            dma((n,)), dma((n,)),
+            dma((n, chips)), dma((n, chips)),
+            dma((n, chips - 1)), dma((n, chips - 1)),
+            dma((n, chips)), dma((n, chips)),
+            dma((n, chips - 1)), dma((n, chips - 1)),
+            dma((n,)), dma((n,)),
+        ],
+        compiler_params=pltpu.CompilerParams(collective_id=1, has_side_effects=True),
+        name="mix_experts",
+    )(normed, state, pick, pick.T, w_in[0], w_out[0])
+
+
+def plain_project(context, residual, master, grad, moment, second, gain):
     model_width = residual.shape[1]
-    half_width = model_width // 2
-    capacity = max(2, 5 * tok_count // (4 * experts))
     fresh = adam_weight(master, grad, moment, second)
     weight_all = lax.all_gather(fresh, "dp", axis=1, tiled=True)
     weight_rows = weight_all.reshape(-1, model_width)
@@ -60,9 +375,13 @@
     ).astype(jnp.float32)
     state = residual.astype(jnp.float32) + attn
     scale = lax.rsqrt(jnp.mean(state * state, axis=-1, keepdims=True) + eps_norm)
-    normed = (state * scale * gain).astype(jnp.bfloat16)
+    return state, (state * scale * gain).astype(jnp.bfloat16)
+
+
+def plain_mix(experts, capacity, state, normed, routes, w_in, w_out):
+    tok_count, model_width = state.shape
+    half_width = model_width // 2
     halves = normed.reshape(tok_count, 2, half_width)
-    routes = jnp.stack([table_one[token_ids], table_two[token_ids]])
     dispatch = slot_tables(routes, experts, capacity)
     outgoing = jnp.einsum(
         "kest,tkd->eksd", dispatch, halves, preferred_element_type=jnp.float32
@@ -82,13 +401,30 @@
     shaped = expert_out.reshape(experts, 2, capacity, half_width)
     returned = lax.all_to_all(shaped, "dp", split_axis=0, concat_axis=0, tiled=True)
     routed = jnp.einsum("kest,eksd->tkd", dispatch, returned, preferred_element_type=jnp.float32)
-    routed = routed.reshape(tok_count, model_width)
-    return (state + routed).astype(jnp.bfloat16)
+    return (state + routed.reshape(tok_count, model_width)).astype(jnp.bfloat16)
+
+
+def on_device(
+    n, exp_size,
+    residual, context, master, grad, moment, second, gain, token_ids, table_one, table_two, w_in, w_out,
+):
+    experts = n * w_in.shape[0]
+    tok_count = residual.shape[0]
+    capacity = max(2, 5 * tok_count // (4 * experts))
+    even = n % 2 == 0 and exp_size % 2 == 0 and n > 2 and exp_size > 2
+    routes = jnp.stack([table_one[token_ids], table_two[token_ids]])
+    if even and master.shape[1] % 16 == 0 and tok_count % 128 == 0 and residual.shape[1] % 512 == 0:
+        state, normed = project(n, exp_size, context, residual, master, grad, moment, second, gain)
+    else:
+        state, normed = plain_project(context, residual, master, grad, moment, second, gain)
+    if even and (2 * capacity) % 8 == 0 and w_in.shape[0] == 1 and tok_count % 128 == 0:
+        return mix_experts(n, exp_size, capacity, state, normed, routes, w_in, w_out)
+    return plain_mix(experts, capacity, state, normed, routes, w_in, w_out)
 
 
 def solution(mesh):
     return jax.shard_map(
-        on_device,
+        functools.partial(on_device, mesh.shape["dp"], mesh.shape["expert"]),
         mesh=mesh,
         in_specs=(
             P(("dp", "expert"), None),

time: 306 us -> 165 us (0.54)
  waiting for transfers between devices: 188 us -> 0 us
  Pallas kernels: 0 us -> 156 us
  blocking collectives: 59.2 us -> 0 us
  matrix products: 23.6 us -> 0 us
  between operations: 13.3 us -> 0.16 us
  local copies, waits for them, and re-layouts: 15.1 us -> 7.89 us
  other arithmetic: 5.76 us -> 0.56 us
    pallas_call x0 -> x2, Pallas kernels: none -> 156 us  [the longest x1 81.4 us: project(): pl.pallas_call(functools.partial(proj_kernel, n, width, exp_size, chunk),...]
    all_gather x2 -> x0, waiting for transfers between devices: 113 us -> none  [the longest x1 82.2 us: on_device(): weight_all = lax.all_gather(fresh, 'dp', axis=1, tiled=True)]
    all_to_all x2 -> x0, blocking collectives: 59.2 us -> none  [the longest x1 29.6 us: on_device(): lax.all_to_all(shaped, 'dp', split_axis=0, concat_axis=0, tiled=True)]
    reduce_scatter x1 -> x0, waiting for transfers between devices: 43.1 us -> none  [on_device(): lax.psum_scatter(partial_rows.astype(jnp.bfloat16), 'expert', scatter_dim...]
    unnamed x5 -> x0, waiting for transfers between devices: 32.3 us -> none
    dot_general x5 -> x0, matrix products: 23.6 us -> none  [the longest x1 9.09 us: on_device(): jnp.dot(lax.all_gather(rows_here, 'expert', axis=0, tiled=True), w_in[0],...]
    convert_element_type x3 -> x1, other arithmetic: 4.81 us -> 0.03 us  [slot_tables(): (match_expert[..., :, None, :] & match_slot[..., None, :, :]).astype(jnp....]
    unnamed x17 -> x10, local copies, waits for them, and re-layouts: 7.39 us -> 3.52 us
  transfers between devices with their start and end apart: 4 -> 0, of which waited for: 4 -> 0; matrix products, arithmetic and copies ran while one was open for 1% -> 0% of each run, Pallas kernels for 0% -> 0%
where the time goes in v1:
time: 165 us; the launch traced here: 164 us
  Pallas kernels  156 us (95%)
  local copies, waits for them, and re-layouts  7.89 us (5%)
    pallas_call x1, Pallas kernels, project(): pl.pallas_call(functools.partial(proj_kernel, n, width, exp_size, chunk),...  81.4 us
    pallas_call x1, Pallas kernels, mix_experts(): pl.pallas_call(functools.partial(moe_kernel, n, exp_size), out_shape=jax....  74.5 us
    unnamed x10, local copies, waits for them, and re-layouts  3.52 us

profile of v1, /device:TPU:0, one launch (start us, length us, event | category | flops | bytes accessed | tf_op | source)
XLA Modules:
  0.0 164.5 jit_solution(6313111491893838123)
XLA Ops:
  0.0 0.0 copy-start
  0.0 1.4 copy.16
  1.5 1.2 copy.17.ctx
  2.6 0.0 copy-start.3
  2.6 0.0 copy-start.2
  2.6 81.4 %project.1 = (f32[128,3072]{1,0:T(8,128)}, bf16[128,3072]{1,0:T(8,128)(2,1)}) custom-call(f32[6,16,3072]{2,1,0:T(8,128)} %master.1, f32[6,16,3072]{2,1,0:T(8,128)} %grad.1, f32[6,16,3072]{2,1,0:T(8,128)} %moment.1, f32[6,16,3072]{2,1,0:T(8,128)} %second.1, bf16[512,768]{1,0:T(8,128)(2,1)} %copy.17.ctx, bf16[128,3072]{1,0:T(8,128)(2,1)} %resid.1, ...), custom_call_target="tpu_custom_call" | custom-call | tf_op jit(solution)/shard_map/project/pallas_call | solution.py:174
  84.0 0.0 copy-done.3
  84.0 0.0 copy-done
  84.0 1.1 gather_fusion.1
  85.2 0.0 copy-done.2
  85.2 1.1 gather_fusion
  86.4 0.1 fusion
  86.5 0.2 reduce_window_sum.11
  86.7 0.2 select_reduce_fusion
  87.1 0.0 copy-start.1
  87.1 0.8 copy.19
  87.9 0.0 copy-done.1
  87.9 74.5 %mix_experts.1 = bf16[128,3072]{1,0:T(8,128)(2,1)} custom-call(bf16[128,3072]{1,0:T(8,128)(2,1)} %get-tuple-element.7.normed, f32[128,3072]{1,0:T(8,128)} %get-tuple-element.8.state, bf16[320,256]{1,0:T(8,128)(2,1)} %copy-done.1, bf16[256,320]{1,0:T(8,128)(2,1)} %bitcast.18, bf16[1536,1280]{1,0:T(8,128)(2,1)} %bitcast.15, bf16[1280,1536]{1,0:T(8,128)(2,1)} %bitcast.16), custom_call_target="tpu_custom_call" | custom-call | tf_op jit(solution)/shard_map/mix_experts/pallas_call | solution.py:344
  162.4 2.1 %copy.21 = bf16[128,3072]{1,0:T(8,128)(2,1)} copy(bf16[128,3072]{1,0:T(8,128)(2,1)} %mix_experts.1) | data formatting | bytes 1572864
  (11 shorter events, 0.2 us)
Async XLA Ops:
  0.0 84.0 %copy-start = (s32[51200]{0:T(1024)S(1)}, s32[51200]{0:T(1024)}, u32[]{:S(2)}) copy-start(s32[51200]{0:T(1024)} %param.21) | copy-start | bytes 614404
  2.6 81.4 %copy-start.3 = (s32[128]{0:T(128)S(1)}, s32[128]{0:T(128)}, u32[]{:S(2)}) copy-start(s32[128]{0:T(128)} %param.19) | copy-start | bytes 1540
  2.6 82.6 %copy-start.2 = (s32[51200]{0:T(1024)S(1)}, s32[51200]{0:T(1024)}, u32[]{:S(2)}) copy-start(s32[51200]{0:T(1024)} %param.20) | copy-start | bytes 614404
  87.1 0.8 copy-start.1
